TPU v7x, 256 devices: a whole 4x4x8 slice. The times are simulated.
256 devices in a mesh: rows: 32 (over z_hi, y, core), cols: 8 (over x, z_lo).
Axes of the slice: x: 4, y: 4, z: 8 (z_hi: 4, z_lo: 2; z = z_hi * 2 + z_lo), core: 2. Of those that a mesh axis runs over, the one named last changes fastest.
Arguments:
- pair: bfloat16 [768, 768, 128], P('rows', 'cols'), may hold values from -6 to 6
- token_mask: int32 [768], P('cols'), may hold values from 0 to 1
- norm_gain: float32 [128], replicated, may hold values from 0.25 to 1.75
- norm_shift: float32 [128], replicated, may hold values from -3 to 3
- in_weight: bfloat16 [128, 512], replicated, may hold values from -1.5 to 1.5
- gate_bias: float32 [128], replicated, may hold values from -4 to 4
- bias_weight: bfloat16 [128, 4], replicated, may hold values from -16 to 16
- out_weight: bfloat16 [128, 128], replicated, may hold values from -1.5 to 1.5
- out_bias: float32 [128], replicated, may hold values from -1.8 to 1.8
Outputs:
- updated: bfloat16 [768, 768, 128], P('rows', 'cols')
All inputs are finite; a program needn't handle non-finite values.
Results may differ from a plain program's by a relative error of at most 0.006.
The roundings to bfloat16 on the way count: a program that leaves them out, or rounds other values in their place, can miss the bound.
Values may be sent and summed in bfloat16 or wider, within the bound.
A program may use at most 128 MiB of HBM per device.

v0:
```python
import jax
import jax.numpy as jnp
from jax import lax
from jax.sharding import PartitionSpec as P


def broadcast(x, axis, root):
    mine = lax.axis_index(axis) == root
    return lax.psum(jnp.where(mine, x, jnp.zeros_like(x)), axis)


def layer_norm(pair_block, norm_gain, norm_shift):
    as_float = pair_block.astype(jnp.float32)
    center = jnp.mean(as_float, axis=-1, keepdims=True)
    spread = jnp.mean(jnp.square(as_float - center), axis=-1, keepdims=True)
    return ((as_float - center) * lax.rsqrt(spread + 1e-05) * norm_gain + norm_shift).astype(
        jnp.bfloat16
    )


def shards(
    pair, token_mask, norm_gain, norm_shift, in_weight, gate_bias, bias_weight, out_weight, out_bias
):
    row_count, col_count, channels = pair.shape
    head_count = bias_weight.shape[1]
    inner_width = out_weight.shape[0]
    head_size = inner_width // head_count
    normed = layer_norm(pair, norm_gain, norm_shift)
    flat_normed = normed.reshape(row_count * col_count, channels)
    bias_tile = jnp.einsum(
        "jkc,ch->jhk", normed, bias_weight, preferred_element_type=jnp.float32
    ).astype(jnp.bfloat16)
    bias_rows_all = lax.all_gather(bias_tile, "cols", axis=2, tiled=True)
    groups = lax.axis_size("rows") // lax.axis_size("cols")
    first_root = lax.axis_index("cols") * groups
    pieces = []
    for offset in range(groups):
        pieces.append(broadcast(bias_rows_all, "rows", first_root + offset))
    own_bias = jnp.concatenate(pieces, axis=0)
    query_gate = jnp.concatenate(
        (in_weight[:, :inner_width], in_weight[:, 3 * inner_width :]), axis=1
    )
    projected = jnp.dot(flat_normed, query_gate, preferred_element_type=jnp.float32)
    queries = (projected[:, :inner_width] * head_size ** (-0.5)).astype(jnp.bfloat16)
    queries = queries.reshape(row_count, col_count, head_count, head_size)
    gates = jax.nn.sigmoid(projected[:, inner_width:] + gate_bias)
    key_value_weight = in_weight[:, inner_width : 3 * inner_width]
    mask_row = token_mask.reshape(1, col_count)
    start_state = (
        jnp.full((row_count, col_count, head_count), -jnp.inf, jnp.float32),
        jnp.zeros((row_count, col_count, head_count), jnp.float32),
        jnp.zeros((row_count, col_count, inner_width), jnp.float32),
    )
    key_values = jnp.dot(flat_normed, key_value_weight, preferred_element_type=jnp.float32).astype(
        jnp.bfloat16
    )
    key_values = key_values.reshape(row_count, col_count, 2 * inner_width)
    pair_keys = lax.all_gather(key_values, "cols", axis=1, tiled=True)
    mask_in = lax.all_gather(mask_row, "cols", axis=1, tiled=True)
    state_now = start_state
    begin_at = jnp.int32(0)
    span_len = pair_keys.shape[1]
    for low_edge in range(0, span_len, col_count):
        high_edge = min(low_edge + col_count, span_len)
        attend_pair_keys = pair_keys[:, low_edge:high_edge]
        attend_begin_at = begin_at + low_edge
        attend_running_max, attend_totals, attend_summed = state_now
        attend_span_len = attend_pair_keys.shape[1]
        key_part = attend_pair_keys[..., :inner_width].reshape(
            row_count, attend_span_len, head_count, head_size
        )
        value_part = attend_pair_keys[..., inner_width:].reshape(
            row_count, attend_span_len, head_count, head_size
        )
        scores = jnp.einsum(
            "rjhd,rkhd->rjhk", queries, key_part, preferred_element_type=jnp.float32
        )
        bias_part = lax.dynamic_slice_in_dim(own_bias, attend_begin_at, attend_span_len, 2).astype(
            jnp.float32
        )
        masking = 1000000000.0 * (mask_in[:, low_edge:high_edge][0].astype(jnp.float32) - 1.0)
        scores = scores + bias_part + masking
        new_max = jnp.maximum(attend_running_max, jnp.max(scores, axis=-1))
        shrink = jnp.exp(attend_running_max - new_max)
        weights = jnp.exp(scores - new_max[..., None])
        attend_totals = attend_totals * shrink + jnp.sum(weights, axis=-1)
        mixed_part = jnp.einsum(
            "rjhk,rkhd->rjhd",
            weights.astype(jnp.bfloat16),
            value_part,
            preferred_element_type=jnp.float32,
        )
        attend_summed = (
            attend_summed.reshape(row_count, col_count, head_count, head_size) * shrink[..., None]
            + mixed_part
        )
        state_now = (
            new_max,
            attend_totals,
            attend_summed.reshape(row_count, col_count, inner_width),
        )
    running_max, totals, summed = state_now
    attended = summed.reshape(row_count, col_count, head_count, head_size) / totals[..., None]
    gated = gates.reshape(row_count, col_count, head_count, head_size) * attended
    gated = gated.astype(jnp.bfloat16).reshape(row_count * col_count, inner_width)
    updated = jnp.dot(gated, out_weight, preferred_element_type=jnp.float32) + out_bias
    return updated.astype(jnp.bfloat16).reshape(row_count, col_count, channels)


def solution(mesh):
    placed = (P("rows", "cols", None), P("cols"), P(), P(), P(), P(), P(), P(), P())
    return jax.shard_map(
        shards, mesh=mesh, in_specs=placed, out_specs=P("rows", "cols", None), check_vma=False
    )
```

profile of v0, /device:TPU:2, one launch (start us, length us, event | category | flops | bytes accessed | tf_op | source)
XLA Modules:
  0.0 610.0 jit_solution(3657278403841043322)
XLA Ops:
  13.8 30.4 %all_gather.10 = bf16[24,4,768]{0,1,2:T(4,128)(2,1)S(1)} all-gather(bf16[24,4,96]{0,1,2:T(4,128)(2,1)S(1)} %copy.144), channel_id=1, replica_groups=mesh['rows'=32,'cols'=8] {'cols'}, dimensions={2}, use_global_device_ids=true | all-gather | bytes 165888 | tf_op jit(solution)/shard_map/all_gather | solution.py:33
  51.0 10.0 %all-reduce = s32[768]{0:T(1024)S(1)} all-reduce(s32[768]{0:T(1024)S(1)} %dynamic-update-slice), channel_id=2, replica_groups=mesh['rows'=32,'cols'=8] {'cols'}, use_global_device_ids=true, to_apply=%add | all-reduce | flops 768 | bytes 6144
  62.4 2.4 reshape.407
  64.9 406.6 %all-reduce.4.cloned.1.call-done = (bf16[24,4,768]{2,0,1:T(8,128)(2,1)}, bf16[24,4,768]{2,0,1:T(8,128)(2,1)}, bf16[24,4,768]{2,0,1:T(8,128)(2,1)}, bf16[24,4,768]{2,0,1:T(8,128)(2,1)}) async-done(((bf16[24,4,768]{2,0,1:T(8,128)(2,1)}, bf16[24,4,768]{2,0,1:T(8,128)(2,1)}, bf16[24,4,768]{2,0,1:T(8,128)(2,1)}, bf16[24,4,768]{2,0,1:T(8,128)(2,1)}), (bf16[24,4,768]{2,0,1:T(8,128)(2,1)}, ...) | async-done | bytes 589840 | tf_op jit(solution)/shard_map/psum | solution.py:9
  484.6 7.4 %fusion.145 = (bf16[24,96,128]{2,1,0:T(8,128)(2,1)}, bf16[24,96,128]{2,1,0:T(8,128)(2,1)}, bf16[24,96,128]{2,1,0:T(8,128)(2,1)S(1)}, bf16[24,96,128]{2,1,0:T(8,1...) fusion(bf16[24,768,256]{2,1,0:T(8,128)(2,1)} %all-gather.3.clon, ...), kind=kLoop, calls=%fused_computation.201 | loop fusion | bytes 18874368 | tf_op jit(solution)/shard_map/slice | solution.py:72
  492.0 2.2 copy.167
  494.2 2.3 copy.162
  505.4 2.2 copy.177
  510.3 4.6 fusion.29
  514.9 3.5 fusion.28
  518.4 3.4 fusion.27
  525.1 3.5 fusion.30
  528.6 3.5 fusion.31
  532.1 3.4 fusion.32
  536.2 4.2 fusion.8
  544.5 4.7 fusion.43
  549.2 6.5 %fusion.12 = (f32[24,96,4]{1,2,0:T(4,128)}, f32[24,96,4]{1,2,0:T(4,128)}) fusion(f32[24,4,96,96]{3,2,1,0:T(8,128)} %get-tuple-element.76, f32[24,96,4]{1,2,0:T(4,128)S(1)} %bitcast.267, f32[96]{0:T(128)S(1)} %get-tuple-element.63, f32[96,4,96]{0,2,1:T(8,128)S(1)} %copy-done.19, f32[24,96,4]{1,2,0:T(4,128)S(1)} %bitcast.263, f32[96]{0:T(128)S(1)} %get-tuple-element.62, ...), kind=kLoop, calls=%fused_computation.28 | loop fusion | flops 7059456 | bytes 7521024 | tf_op jit(solution)/shard_map/reduce_sum | solution.py:86
  555.7 2.3 fusion.41
  560.9 4.8 fusion.39
  565.7 6.7 %fusion.16 = (f32[24,96,4]{1,2,0:T(4,128)}, f32[24,96,4]{1,2,0:T(4,128)}) fusion(f32[24,4,96,96]{3,2,1,0:T(8,128)} %get-tuple-element.72, f32[24,96,4]{1,2,0:T(4,128)S(1)} %bitcast.261, f32[96]{0:T(128)S(1)} %get-tuple-element.61, f32[96,4,96]{0,2,1:T(8,128)S(1)} %copy-done.13, f32[24,96,4]{1,2,0:T(4,128)S(1)} %bitcast.257, f32[96]{0:T(128)S(1)} %get-tuple-element.60, ...), kind=kLoop, calls=%fused_computation.32 | loop fusion | flops 7059456 | bytes 7521024 | tf_op jit(solution)/shard_map/reduce_sum | solution.py:86
  572.4 2.3 fusion.37
  577.6 4.7 fusion.35
  582.2 6.3 %fusion.20 = (f32[24,96,4]{1,2,0:T(4,128)}, f32[24,96,4]{1,2,0:T(4,128)}) fusion(f32[24,4,96,96]{3,2,1,0:T(8,128)} %get-tuple-element.68, f32[24,96,4]{1,2,0:T(4,128)S(1)} %bitcast.255, f32[96]{0:T(128)S(1)} %get-tuple-element.59, f32[96,4,96]{0,2,1:T(8,128)S(1)} %copy-done.12, f32[24,96,4]{1,2,0:T(4,128)S(1)} %bitcast.251, f32[96]{0:T(128)S(1)} %get-tuple-element.58, ...), kind=kLoop, calls=%fused_computation.36 | loop fusion | flops 7059456 | bytes 7521024 | tf_op jit(solution)/shard_map/reduce_sum | solution.py:86
  592.5 7.6 %fusion.75 = bf16[24,96,4,32]{1,3,2,0:T(8,128)(2,1)S(1)} fusion(f32[24,4,32,96]{3,2,1,0:T(8,128)} %fusion.33, f32[24,4,32,96]{3,2,1,0:T(8,128)} %fusion.35, f32[24,4,32,96]{3,2,1,0:T(8,128)} %fusion.37, f32[24,4,32,96]{3,2,1,0:T(8,128)} %fusion.39, f32[24,4,32,96]{3,2,1,0:T(8,128)} %fusion.41, f32[24,4,32,96]{3,2,1,0:T(8,128)} %fusion.43, ...), kind=kOutput, calls=%fused_computation.86 | convolution fusion | flops 65470464 | bytes 14672256 | tf_op jit(solution)/shard_map/rjhk,rkhd->rjhd/dot_general | solution.py:87
  (150 shorter events, 58.3 us)
Async XLA Ops:
  7.4 593.8 %copy-start = (bf16[128,128]{1,0:T(8,128)(2,1)S(1)}, bf16[128,128]{1,0:T(8,128)(2,1)}, u32[]{:S(2)}) copy-start(bf16[128,128]{1,0:T(8,128)(2,1)} %param.16) | copy-start | bytes 98308
  7.4 38.2 %copy-start.32 = (bf16[128,512]{1,0:T(8,128)(2,1)S(1)}, bf16[128,512]{1,0:T(8,128)(2,1)}, u32[]{:S(2)}) copy-start(bf16[128,512]{1,0:T(8,128)(2,1)} %param.13) | copy-start | bytes 393220
  7.4 464.1 %all-reduce.4.cloned.1.call-start = ((), (), s32[]{:S(2)}) async-start(), calls=%async_computation.1 | async-start | bytes 1179648 | tf_op jit(solution)/shard_map/psum | solution.py:9
  13.6 34.0 %copy-start.33 = (f32[128]{0:T(128)S(1)}, f32[128]{0:T(128)}, u32[]{:S(2)}) copy-start(f32[128]{0:T(128)} %param.14) | copy-start | bytes 1540
  45.5 439.0 %all-gather.3.cloned.1.call-start = ((), (), s32[]{:S(2)}) async-start(), calls=%async_computation | async-start | bytes 10616832 | tf_op jit(solution)/shard_map/all_gather | solution.py:58
  510.3 4.6 copy-start.8
  523.2 13.0 %copy-start.1 = (f32[24,4,96,96]{3,2,1,0:T(8,128)}, f32[24,4,96,96]{3,2,1,0:T(8,128)S(1)}, u32[]{:S(2)}) copy-start(f32[24,4,96,96]{3,2,1,0:T(8,128)S(1)} %get-tuple-element.78) | copy-start | bytes 10616836
  544.4 4.8 copy-start.17
  544.4 4.8 copy-start.19
  544.4 4.8 copy-start.27
  544.4 4.8 copy-start.29
  544.5 11.2 %slice-start.4 = ((s8[4718592]{0:T(1024)(128)(4,1)}), s8[4194304]{0:T(1024)(128)(4,1)S(1)}, s32[]{:S(2)}) async-start(s8[4718592]{0:T(1024)(128)(4,1)} %bitcast.229), calls=%async_computation.6 | async-start | bytes 8388608
  549.2 6.5 %slice-start.5 = ((s8[4718592]{0:T(1024)(128)(4,1)}), s8[524288]{0:T(1024)(128)(4,1)S(1)}, s32[]{:S(2)}) async-start(s8[4718592]{0:T(1024)(128)(4,1)} %bitcast.229), calls=%async_computation.7 | async-start | bytes 1048576
  560.8 4.8 copy-start.13
  560.9 4.8 copy-start.15
  560.9 4.8 copy-start.23
  560.9 4.8 copy-start.25
  560.9 11.5 %slice-start.2 = ((s8[4718592]{0:T(1024)(128)(4,1)}), s8[4194304]{0:T(1024)(128)(4,1)S(1)}, s32[]{:S(2)}) async-start(s8[4718592]{0:T(1024)(128)(4,1)} %bitcast.227), calls=%async_computation.4 | async-start | bytes 8388608
  565.7 6.7 %slice-start.3 = ((s8[4718592]{0:T(1024)(128)(4,1)}), s8[524288]{0:T(1024)(128)(4,1)S(1)}, s32[]{:S(2)}) async-start(s8[4718592]{0:T(1024)(128)(4,1)} %bitcast.227), calls=%async_computation.5 | async-start | bytes 1048576
  577.5 4.7 copy-start.10
  577.5 4.7 copy-start.12
  577.5 11.1 %slice-start = ((s8[4718592]{0:T(1024)(128)(4,1)}), s8[4194304]{0:T(1024)(128)(4,1)S(1)}, s32[]{:S(2)}) async-start(s8[4718592]{0:T(1024)(128)(4,1)} %bitcast.225), calls=%async_computation.2 | async-start | bytes 8388608
  582.2 6.4 %slice-start.1 = ((s8[4718592]{0:T(1024)(128)(4,1)}), s8[524288]{0:T(1024)(128)(4,1)S(1)}, s32[]{:S(2)}) async-start(s8[4718592]{0:T(1024)(128)(4,1)} %bitcast.225), calls=%async_computation.3 | async-start | bytes 1048576
  592.5 8.7 %copy-start.34 = (f32[128]{0:T(128)S(1)}, f32[128]{0:T(128)}, u32[]{:S(2)}) copy-start(f32[128]{0:T(128)} %param.17) | copy-start | bytes 1540
  (21 other events, 61.9 us)
Sparse Core Ops, SparseCore 0:
  45.7 425.7 all-reduce.3
Sparse Core Ops, SparseCore 1:
  47.8 195.4 all-gather.2
where the time goes:
time: 617 us; the launch traced here: 610 us
  waiting for transfers between devices  407 us (66%)
  matrix products  59.2 us (10%)
  local copies, waits for them, and re-layouts  54.4 us (9%)
  blocking collectives  40.4 us (7%)
  other arithmetic  32.8 us (5%)
  between operations  16.5 us (3%)
    psum x1, waiting for transfers between devices, broadcast(): return lax.psum(jnp.where(mine, x, jnp.zeros_like(x)), axis)  407 us
    dot_general x8, matrix products, shards(): jnp.einsum('rjhk,rkhd->rjhd', weights.astype(jnp.bfloat16), value_part, p...  30.7 us
    all_gather x1, blocking collectives, shards(): bias_rows_all = lax.all_gather(bias_tile, 'cols', axis=2, tiled=True)  30.4 us
    dot_general x8, matrix products, shards(): jnp.einsum('rjhd,rkhd->rjhk', queries, key_part, preferred_element_type=j...  24.3 us
    reduce_sum x4, other arithmetic, shards(): attend_totals = attend_totals * shrink + jnp.sum(weights, axis=-1)  23.7 us
    slice x8, local copies, waits for them, and re-layouts, shards(): attend_pair_keys[..., :inner_width]  16.8 us
    slice x9, local copies, waits for them, and re-layouts, shards(): attend_pair_keys[..., inner_width:]  16.8 us
  transfers between devices with their start and end apart: 2, of which 1 were waited for; matrix products, arithmetic and copies ran while one was open for 4% of the time, Pallas kernels for 0%

commit v1 on v0

--- a/solution.py
+++ b/solution.py
@@ -30,7 +30,9 @@
     bias_tile = jnp.einsum(
         "jkc,ch->jhk", normed, bias_weight, preferred_element_type=jnp.float32
     ).astype(jnp.bfloat16)
-    bias_rows_all = lax.all_gather(bias_tile, "cols", axis=2, tiled=True)
+    bias_rows_all = jnp.concatenate(
+        lax.all_to_all(jnp.stack([bias_tile] * lax.axis_size("cols")), "cols", 0, 0), axis=2
+    )
     groups = lax.axis_size("rows") // lax.axis_size("cols")
     first_root = lax.axis_index("cols") * groups
     pieces = []

time: 617 us -> 600 us (0.972)
  blocking collectives: 40.4 us -> 9.74 us
  starting transfers between devices: 0.05 us -> 6.23 us
    all_gather x1 -> x0, blocking collectives: 30.4 us -> none  [shards(): bias_rows_all = lax.all_gather(bias_tile, 'cols', axis=2, tiled=True)]
    all_to_all x0 -> x1, starting transfers between devices: none -> 6.18 us  [shards(): lax.all_to_all(jnp.stack([bias_tile] * lax.axis_size('cols')), 'cols', 0, 0)]
  transfers between devices with their start and end apart: 2 -> 3, of which waited for: 1 -> 2; matrix products, arithmetic and copies ran while one was open for 4% -> 4% of each run, Pallas kernels for 0% -> 0%
where the time goes in v1:
time: 600 us; the launch traced here: 592 us
  waiting for transfers between devices  411 us (68%)
  matrix products  59.3 us (10%)
  local copies, waits for them, and re-layouts  57.9 us (10%)
  other arithmetic  32 us (5%)
  between operations  16.4 us (3%)
  blocking collectives  9.74 us (2%)
  starting transfers between devices  6.23 us (1%)
    psum x1, waiting for transfers between devices, broadcast(): return lax.psum(jnp.where(mine, x, jnp.zeros_like(x)), axis)  406 us
    dot_general x8, matrix products, shards(): jnp.einsum('rjhk,rkhd->rjhd', weights.astype(jnp.bfloat16), value_part, p...  30.7 us
    dot_general x8, matrix products, shards(): jnp.einsum('rjhd,rkhd->rjhk', queries, key_part, preferred_element_type=j...  24.4 us
    reduce_sum x4, other arithmetic, shards(): attend_totals = attend_totals * shrink + jnp.sum(weights, axis=-1)  23.7 us
    slice x9, local copies, waits for them, and re-layouts, shards(): attend_pair_keys[..., inner_width:]  16.8 us
    slice x8, local copies, waits for them, and re-layouts, shards(): attend_pair_keys[..., :inner_width]  16.8 us
  transfers between devices with their start and end apart: 3, of which 2 were waited for; matrix products, arithmetic and copies ran while one was open for 4% of the time, Pallas kernels for 0%

profile of v1, /device:TPU:2, one launch (start us, length us, event | category | flops | bytes accessed | tf_op | source)
XLA Modules:
  0.0 592.5 jit_solution(15681417198937394604)
XLA Ops:
  14.3 6.2 %all-to-all-start = ((bf16[8,24,4,96]{3,1,2,0:T(8,128)(2,1)}), bf16[8,24,4,96]{3,1,2,0:T(8,128)(2,1)S(1)}, u32[]{:S(2)}, u32[]{:S(2)}) async-start(bf16[8,24,4,96]{3,1,2,0:T(8,128)(2,1)} %stack.2), calls=%async_computation | async-start | bytes 393216 | tf_op jit(solution)/shard_map/all_to_all | solution.py:34
  20.5 5.2 all-to-all-done
  34.9 9.7 %all-reduce = s32[768]{0:T(1024)S(1)} all-reduce(s32[768]{0:T(1024)S(1)} %dynamic-update-slice), channel_id=2, replica_groups=mesh['rows'=32,'cols'=8] {'cols'}, use_global_device_ids=true, to_apply=%add | all-reduce | flops 768 | bytes 6144
  46.0 2.3 reshape.423
  48.4 405.6 %all-reduce.4.cloned.1.call-done = (bf16[24,4,768]{2,0,1:T(8,128)(2,1)}, bf16[24,4,768]{2,0,1:T(8,128)(2,1)}, bf16[24,4,768]{2,0,1:T(8,128)(2,1)}, bf16[24,4,768]{2,0,1:T(8,128)(2,1)}) async-done(((bf16[24,4,768]{2,0,1:T(8,128)(2,1)}, bf16[24,4,768]{2,0,1:T(8,128)(2,1)}, bf16[24,4,768]{2,0,1:T(8,128)(2,1)}, bf16[24,4,768]{2,0,1:T(8,128)(2,1)}), (bf16[24,4,768]{2,0,1:T(8,128)(2,1)}, ...) | async-done | bytes 589840 | tf_op jit(solution)/shard_map/psum | solution.py:9
  467.1 7.4 %fusion.145 = (bf16[24,96,128]{2,1,0:T(8,128)(2,1)}, bf16[24,96,128]{2,1,0:T(8,128)(2,1)}, bf16[24,96,128]{2,1,0:T(8,128)(2,1)S(1)}, bf16[24,96,128]{2,1,0:T(8,1...) fusion(bf16[24,768,256]{2,1,0:T(8,128)(2,1)} %all-gather.3.clon, ...), kind=kLoop, calls=%fused_computation.201 | loop fusion | bytes 18874368 | tf_op jit(solution)/shard_map/slice | solution.py:74
  476.7 2.2 copy.140
  487.8 2.2 copy.155
  492.7 4.6 fusion.29
  497.4 3.5 fusion.28
  500.9 3.4 fusion.27
  507.5 3.4 fusion.30
  511.0 3.5 fusion.31
  514.5 3.4 fusion.32
  518.6 4.2 fusion.8
  526.9 4.7 fusion.43
  531.7 6.5 %fusion.12 = (f32[24,96,4]{1,2,0:T(4,128)}, f32[24,96,4]{1,2,0:T(4,128)}) fusion(f32[24,4,96,96]{3,2,1,0:T(8,128)} %get-tuple-element.76, f32[24,96,4]{1,2,0:T(4,128)S(1)} %bitcast.291, f32[96]{0:T(128)S(1)} %get-tuple-element.63, f32[96,4,96]{0,2,1:T(8,128)S(1)} %copy-done.19, f32[24,96,4]{1,2,0:T(4,128)S(1)} %bitcast.287, f32[96]{0:T(128)S(1)} %get-tuple-element.62, ...), kind=kLoop, calls=%fused_computation.28 | loop fusion | flops 7059456 | bytes 7521024 | tf_op jit(solution)/shard_map/reduce_sum | solution.py:88
  538.1 2.3 fusion.41
  543.3 4.8 fusion.39
  548.1 6.7 %fusion.16 = (f32[24,96,4]{1,2,0:T(4,128)}, f32[24,96,4]{1,2,0:T(4,128)}) fusion(f32[24,4,96,96]{3,2,1,0:T(8,128)} %get-tuple-element.72, f32[24,96,4]{1,2,0:T(4,128)S(1)} %bitcast.285, f32[96]{0:T(128)S(1)} %get-tuple-element.61, f32[96,4,96]{0,2,1:T(8,128)S(1)} %copy-done.13, f32[24,96,4]{1,2,0:T(4,128)S(1)} %bitcast.281, f32[96]{0:T(128)S(1)} %get-tuple-element.60, ...), kind=kLoop, calls=%fused_computation.32 | loop fusion | flops 7059456 | bytes 7521024 | tf_op jit(solution)/shard_map/reduce_sum | solution.py:88
  554.8 2.3 fusion.37
  560.0 4.7 fusion.35
  564.7 6.3 %fusion.20 = (f32[24,96,4]{1,2,0:T(4,128)}, f32[24,96,4]{1,2,0:T(4,128)}) fusion(f32[24,4,96,96]{3,2,1,0:T(8,128)} %get-tuple-element.68, f32[24,96,4]{1,2,0:T(4,128)S(1)} %bitcast.279, f32[96]{0:T(128)S(1)} %get-tuple-element.59, f32[96,4,96]{0,2,1:T(8,128)S(1)} %copy-done.12, f32[24,96,4]{1,2,0:T(4,128)S(1)} %bitcast.275, f32[96]{0:T(128)S(1)} %get-tuple-element.58, ...), kind=kLoop, calls=%fused_computation.36 | loop fusion | flops 7059456 | bytes 7521024 | tf_op jit(solution)/shard_map/reduce_sum | solution.py:88
  574.9 7.6 %fusion.75 = bf16[24,96,4,32]{1,3,2,0:T(8,128)(2,1)S(1)} fusion(f32[24,4,32,96]{3,2,1,0:T(8,128)} %fusion.33, f32[24,4,32,96]{3,2,1,0:T(8,128)} %fusion.35, f32[24,4,32,96]{3,2,1,0:T(8,128)} %fusion.37, f32[24,4,32,96]{3,2,1,0:T(8,128)} %fusion.39, f32[24,4,32,96]{3,2,1,0:T(8,128)} %fusion.41, f32[24,4,32,96]{3,2,1,0:T(8,128)} %fusion.43, ...), kind=kOutput, calls=%fused_computation.86 | convolution fusion | flops 65470464 | bytes 14672256 | tf_op jit(solution)/shard_map/rjhk,rkhd->rjhd/dot_general | solution.py:89
  (159 shorter events, 63.4 us)
Async XLA Ops:
  7.4 576.3 %copy-start = (bf16[128,128]{1,0:T(8,128)(2,1)S(1)}, bf16[128,128]{1,0:T(8,128)(2,1)}, u32[]{:S(2)}) copy-start(bf16[128,128]{1,0:T(8,128)(2,1)} %param.16) | copy-start | bytes 98308
  7.4 22.2 %copy-start.32 = (bf16[128,512]{1,0:T(8,128)(2,1)S(1)}, bf16[128,512]{1,0:T(8,128)(2,1)}, u32[]{:S(2)}) copy-start(bf16[128,512]{1,0:T(8,128)(2,1)} %param.13) | copy-start | bytes 393220
  14.3 11.4 %all-to-all-start = ((bf16[8,24,4,96]{3,1,2,0:T(8,128)(2,1)}), bf16[8,24,4,96]{3,1,2,0:T(8,128)(2,1)S(1)}, u32[]{:S(2)}, u32[]{:S(2)}) async-start(bf16[8,24,4,96]{3,1,2,0:T(8,128)(2,1)} %stack.2), calls=%async_computation | async-start | bytes 393216 | tf_op jit(solution)/shard_map/all_to_all | solution.py:34
  20.5 433.5 %all-reduce.4.cloned.1.call-start = ((), (), s32[]{:S(2)}) async-start(), calls=%async_computation.2 | async-start | bytes 1179648 | tf_op jit(solution)/shard_map/psum | solution.py:9
  25.9 5.7 copy-start.33
  29.5 437.5 %all-gather.3.cloned.1.call-start = ((), (), s32[]{:S(2)}) async-start(), calls=%async_computation.1 | async-start | bytes 10616832 | tf_op jit(solution)/shard_map/all_gather | solution.py:60
  505.6 13.0 %copy-start.1 = (f32[24,4,96,96]{3,2,1,0:T(8,128)}, f32[24,4,96,96]{3,2,1,0:T(8,128)S(1)}, u32[]{:S(2)}) copy-start(f32[24,4,96,96]{3,2,1,0:T(8,128)S(1)} %get-tuple-element.78) | copy-start | bytes 10616836
  526.9 4.8 copy-start.17
  526.9 4.8 copy-start.19
  526.9 4.7 copy-start.27
  526.9 4.7 copy-start.29
  526.9 11.2 %slice-start.4 = ((s8[4718592]{0:T(1024)(128)(4,1)}), s8[4194304]{0:T(1024)(128)(4,1)S(1)}, s32[]{:S(2)}) async-start(s8[4718592]{0:T(1024)(128)(4,1)} %bitcast.253), calls=%async_computation.7 | async-start | bytes 8388608
  531.6 6.5 %slice-start.5 = ((s8[4718592]{0:T(1024)(128)(4,1)}), s8[524288]{0:T(1024)(128)(4,1)S(1)}, s32[]{:S(2)}) async-start(s8[4718592]{0:T(1024)(128)(4,1)} %bitcast.253), calls=%async_computation.8 | async-start | bytes 1048576
  543.3 4.8 copy-start.13
  543.3 4.8 copy-start.15
  543.3 4.8 copy-start.23
  543.3 4.8 copy-start.25
  543.3 11.5 %slice-start.2 = ((s8[4718592]{0:T(1024)(128)(4,1)}), s8[4194304]{0:T(1024)(128)(4,1)S(1)}, s32[]{:S(2)}) async-start(s8[4718592]{0:T(1024)(128)(4,1)} %bitcast.251), calls=%async_computation.5 | async-start | bytes 8388608
  548.1 6.7 %slice-start.3 = ((s8[4718592]{0:T(1024)(128)(4,1)}), s8[524288]{0:T(1024)(128)(4,1)S(1)}, s32[]{:S(2)}) async-start(s8[4718592]{0:T(1024)(128)(4,1)} %bitcast.251), calls=%async_computation.6 | async-start | bytes 1048576
  560.0 4.7 copy-start.10
  560.0 4.7 copy-start.12
  560.0 11.1 %slice-start = ((s8[4718592]{0:T(1024)(128)(4,1)}), s8[4194304]{0:T(1024)(128)(4,1)S(1)}, s32[]{:S(2)}) async-start(s8[4718592]{0:T(1024)(128)(4,1)} %bitcast.249), calls=%async_computation.3 | async-start | bytes 8388608
  564.7 6.4 %slice-start.1 = ((s8[4718592]{0:T(1024)(128)(4,1)}), s8[524288]{0:T(1024)(128)(4,1)S(1)}, s32[]{:S(2)}) async-start(s8[4718592]{0:T(1024)(128)(4,1)} %bitcast.249), calls=%async_computation.4 | async-start | bytes 1048576
  574.9 8.7 %copy-start.34 = (f32[128]{0:T(128)S(1)}, f32[128]{0:T(128)}, u32[]{:S(2)}) copy-start(f32[128]{0:T(128)} %param.17) | copy-start | bytes 1540
  (22 other events, 66.4 us)
Sparse Core Ops, SparseCore 0:
  29.6 424.2 all-reduce.3
Sparse Core Ops, SparseCore 1:
  31.8 193.9 all-gather.2
